TPU v7x, 32 devices: a whole 2x2x4 slice. The times are simulated.
32 devices in a mesh: sample: 8 (over y, x, core), chan: 4 (over z).
Axes of the slice: x: 2, y: 2, z: 4, core: 2. Of those that a mesh axis runs over, the one named last changes fastest.
Arguments:
- snapshots: bfloat16 [8, 256, 512], P('sample', None, 'chan'), may hold values from -6 to 6
- first_weight: bfloat16 [256, 27, 256], P('chan'), may hold values from -0.078125 to 0.078125
- second_weight: bfloat16 [256, 27, 256], P('chan'), may hold values from -0.078125 to 0.078125
- cotangent: bfloat16 [8, 256, 512], P('sample', 'chan'), may hold values from -0.09375 to 0.09375
Outputs:
- second_out: bfloat16 [8, 256, 512], P('sample', 'chan')
- first_grad: float32 [256, 27, 256], P('chan', None, 'sample')
- second_grad: float32 [256, 27, 256], P('chan', None, 'sample')
All inputs are finite; a program needn't handle non-finite values.
Results may differ from a plain program's by a relative error of at most 0.0061.
Values may be sent and summed in bfloat16 or wider, within the bound.
No kernel may reach another device: no remote copies, remote signals or barrier semaphores. Data moves between devices by JAX's collectives and lax.ppermute only.
A program may use at most 128 MiB of HBM per device.

v0:
```python
import jax
import jax.numpy as jnp
from jax import lax
from jax.sharding import PartitionSpec as P

SIDE = 8


def shifted(fields):
    batch_size, channels = (fields.shape[0], fields.shape[1])
    cube_form = fields.reshape(batch_size, channels, SIDE, SIDE, SIDE)
    padded = jnp.pad(cube_form, ((0, 0), (0, 0), (1, 1), (1, 1), (1, 1)))
    shifted_views = []
    for tap_index in range(27):
        shift_depth, shift_rows, shift_cols = (tap_index // 9, tap_index // 3 % 3, tap_index % 3)
        shifted_views.append(
            padded[
                :,
                :,
                shift_depth : shift_depth + SIDE,
                shift_rows : shift_rows + SIDE,
                shift_cols : shift_cols + SIDE,
            ]
        )
    return jnp.stack(shifted_views, axis=2).reshape(batch_size, channels * 27, SIDE * SIDE * SIDE)


def spread(terms):
    batch_size, channels = (terms.shape[0], terms.shape[1] // 27)
    cube_form = terms.reshape(batch_size, channels, 27, SIDE, SIDE, SIDE)
    padded = jnp.pad(cube_form, ((0, 0), (0, 0), (0, 0), (1, 1), (1, 1), (1, 1)))
    total = jnp.zeros((batch_size, channels, SIDE, SIDE, SIDE), jnp.float32)
    for tap_index in range(27):
        shift_depth, shift_rows, shift_cols = (tap_index // 9, tap_index // 3 % 3, tap_index % 3)
        total = (
            total
            + padded[
                :,
                :,
                tap_index,
                2 - shift_depth : 2 - shift_depth + SIDE,
                2 - shift_rows : 2 - shift_rows + SIDE,
                2 - shift_cols : 2 - shift_cols + SIDE,
            ]
        )
    return total.reshape(batch_size, channels, SIDE * SIDE * SIDE)


def layer_sums(kernel_rows, patches):
    partial_value = jnp.einsum(
        "kc,bkp->bcp", kernel_rows, patches, preferred_element_type=jnp.float32
    )
    return lax.psum_scatter(partial_value, "chan", scatter_dimension=1, tiled=True)


def all_channels(grad_maps):
    return lax.all_gather(grad_maps, "chan", axis=1, tiled=True)


def body(snapshots, first_weight, second_weight, cotangent):
    channel_maps = lax.all_to_all(snapshots, "chan", split_axis=1, concat_axis=2, tiled=True)
    input_patches = shifted(channel_maps)
    first_rows = first_weight.reshape(-1, first_weight.shape[2])
    second_rows = second_weight.reshape(-1, second_weight.shape[2])
    first_sum = layer_sums(first_rows, input_patches)
    first_map = first_sum.astype(jnp.bfloat16)
    first_values = first_map.astype(jnp.float32)
    hidden = jax.nn.silu(first_values).astype(jnp.bfloat16)
    hidden_patches = shifted(hidden)
    second_out = layer_sums(second_rows, hidden_patches).astype(jnp.bfloat16)
    full_cotangent = all_channels(cotangent)
    second_term = jnp.einsum(
        "bkp,bcp->kc", hidden_patches, full_cotangent, preferred_element_type=jnp.float32
    )
    terms = jnp.einsum(
        "kc,bcp->bkp", second_rows, full_cotangent, preferred_element_type=jnp.float32
    )
    hidden_grad = spread(terms)
    sigmoid_values = jax.nn.sigmoid(first_values)
    first_map_grad = (
        hidden_grad * sigmoid_values * (1.0 + first_values * (1.0 - sigmoid_values))
    ).astype(jnp.bfloat16)
    full_map_grad = all_channels(first_map_grad)
    first_term = jnp.einsum(
        "bkp,bcp->kc", input_patches, full_map_grad, preferred_element_type=jnp.float32
    )
    first_grad, second_grad = (
        lax.psum_scatter(first_term, "sample", scatter_dimension=1, tiled=True),
        lax.psum_scatter(second_term, "sample", scatter_dimension=1, tiled=True),
    )
    return (
        second_out,
        first_grad.reshape(first_weight.shape[0], 27, -1),
        second_grad.reshape(second_weight.shape[0], 27, -1),
    )


def solution(mesh):
    placed = (
        P("sample", None, "chan"),
        P("chan", None, None),
        P("chan", None, None),
        P("sample", "chan", None),
    )
    return jax.shard_map(
        body,
        mesh=mesh,
        in_specs=placed,
        out_specs=(P("sample", "chan", None), P("chan", None, "sample"), P("chan", None, "sample")),
        check_vma=False,
    )
```

profile of v0, /device:TPU:0, one launch (start us, length us, event | category | flops | bytes accessed | tf_op | source)
XLA Modules:
  0.0 640.3 jit_solution(11114681304338015524)
XLA Ops:
  7.2 1.0 copy.72
  8.7 1.0 reduce.22
  10.3 6.3 all-to-all-start
  16.7 1.7 copy.63
  18.3 1.2 reshape.411
  19.5 14.5 %all_gather.6 = bf16[1,256,512]{2,1,0:T(8,128)(2,1)S(1)} all-gather(bf16[1,64,512]{2,1,0:T(8,128)(2,1)S(1)} %copy-done.4), channel_id=1, replica_groups=mesh['sample'=8,'chan'=4] {'chan'}, dimensions={1}, use_global_device_ids=true | all-gather | bytes 327680 | tf_op jit(solution)/shard_map/all_gather | solution.py:57
  34.0 0.7 copy-done.1
  34.7 1.8 convolution_bitcast_fusion
  36.5 3.1 copy.65
  39.6 22.4 %reshape.413 = f32[1,64,27,8,8,8]{2,1,5,4,3,0:T(8,128)} reshape(f32[1,1728,512]{1,2,0:T(8,128)} %copy.65) | data formatting | bytes 7077888 | tf_op jit(solution)/shard_map/reshape | solution.py:30
  62.0 178.1 %fusion.16 = (f32[64,8,8,8]{0,3,2,1:T(8,128)S(1)}, f32[64,8,8,8]{0,3,2,1:T(8,128)S(1)}, f32[64,8,8,8]{0,3,2,1:T(8,128)S(1)}, f32[64,8,8,8]{0,3,2,1:T(8,128)S(1)}...) fusion(f32[1,64,27,8,8,8]{2,1,5,4,3,0:T(8,128)} %reshape.413), kind=kLoop, calls=%fused_computation.42 | loop fusion | flops 524288 | bytes 34996224 | tf_op jit(solution)/shard_map/slice | solution.py:37
  240.6 1.2 reshape.408
  243.1 0.9 reshape.443
  253.7 0.7 fusion.66
  262.6 9.5 %copy.58 = bf16[1,64,27,8,8,8]{2,1,5,4,3,0:T(8,128)(2,1)} copy(bf16[1,64,27,8,8,8]{1,5,4,3,2,0:T(8,128)(2,1)} %fusion.90) | data formatting | bytes 3538944 | tf_op jit(solution)/shard_map/stack | solution.py:25
  272.1 11.3 %reshape.407 = bf16[1728,512]{0,1:T(8,128)(2,1)S(1)} reshape(bf16[1,64,27,8,8,8]{2,1,5,4,3,0:T(8,128)(2,1)} %copy.58) | data formatting | bytes 3538944 | tf_op jit(solution)/shard_map/reshape.2
  283.4 2.6 convolution_bitcast_fusion.2
  286.0 1.3 copy.60
  287.3 140.8 %all-reduce.7 = bf16[1,256,512]{2,0,1:T(2,128)(2,1)} all-reduce(f32[1,256,512]{2,0,1:T(1,128)S(1)} %copy.60), channel_id=2, replica_groups=mesh['sample'=8,'chan'=4] {'chan'}, use_global_device_ids=true, to_apply=%region_0.1.clone | all-reduce | flops 131072 | bytes 786432
  428.1 1.0 constant_dynamic-slice_fusion
  429.3 1.6 fusion.33
  435.1 14.1 %all_gather.7 = bf16[1,256,512]{2,1,0:T(8,128)(2,1)S(1)} all-gather(bf16[1,64,512]{2,1,0:T(8,128)(2,1)S(1)} %copy.66), channel_id=1, replica_groups=mesh['sample'=8,'chan'=4] {'chan'}, dimensions={1}, use_global_device_ids=true | all-gather | bytes 327680 | tf_op jit(solution)/shard_map/all_gather | solution.py:57
  449.2 2.0 fusion.34
  456.8 0.7 fusion.118
  465.7 9.6 %copy.62 = bf16[1,64,27,8,8,8]{2,1,5,4,3,0:T(8,128)(2,1)} copy(bf16[1,64,27,8,8,8]{1,5,4,3,2,0:T(8,128)(2,1)} %fusion.142) | data formatting | bytes 3538944 | tf_op jit(solution)/shard_map/stack | solution.py:25
  475.2 11.3 %reshape.410 = bf16[1728,512]{0,1:T(8,128)(2,1)S(1)} reshape(bf16[1,64,27,8,8,8]{2,1,5,4,3,0:T(8,128)(2,1)} %copy.62) | data formatting | bytes 3538944 | tf_op jit(solution)/shard_map/reshape.5
  486.6 1.9 fusion.37
  489.6 136.3 %all-reduce.8 = bf16[1,256,512]{2,0,1:T(2,128)(2,1)S(1)} all-reduce(f32[1,256,512]{2,0,1:T(1,128)S(1)} %copy.64), channel_id=3, replica_groups=mesh['sample'=8,'chan'=4] {'chan'}, use_global_device_ids=true, to_apply=%region_1.2.clone | all-reduce | flops 131072 | bytes 786432
  626.7 2.2 reshape.415
  628.9 1.2 copy.68
  630.1 2.2 reshape.416
  632.3 1.2 copy.69
  (82 shorter events, 40.0 us)
Async XLA Ops:
  7.2 12.4 %copy-start.4 = (bf16[1,64,512]{2,1,0:T(8,128)(2,1)S(1)}, bf16[1,64,512]{2,1,0:T(8,128)(2,1)}, u32[]{:S(2)}) copy-start(bf16[1,64,512]{2,1,0:T(8,128)(2,1)} %param.7) | copy-start | bytes 196612
  10.3 232.7 %all-to-all-start = ((bf16[4,2,4096]{2,1,0:T(2,128)(2,1)}), bf16[4,2,4096]{2,1,0:T(2,128)(2,1)}, u32[]{:S(2)}, u32[]{:S(2)}) async-start(bf16[4,2,4096]{2,1,0:T(2,128)(2,1)} %reshape.442), calls=%async_computation | async-start | bytes 131072 | tf_op jit(solution)/shard_map/all_to_all | solution.py:61
  16.6 610.1 %reduce-scatter.3.cloned.1.call-start = ((), (), s32[]{:S(2)}) async-start(), calls=%async_computation.3 | async-start | bytes 2064384 | tf_op jit(solution)/shard_map/reduce_scatter | solution.py:88
  34.0 0.7 copy-start.1
  62.0 178.1 %copy-start.3 = (bf16[64,27,256]{2,0,1:T(8,128)(2,1)S(1)}, bf16[64,27,256]{2,0,1:T(8,128)(2,1)}, u32[]{:S(2)}) copy-start(bf16[64,27,256]{2,0,1:T(8,128)(2,1)} %param.5) | copy-start | bytes 2654212
  240.1 1.7 copy-start.5
  451.2 178.8 %reduce-scatter.5.cloned.1.call-start = ((), (), s32[]{:S(2)}) async-start(), calls=%async_computation.4 | async-start | bytes 2064384 | tf_op jit(solution)/shard_map/reduce_scatter | solution.py:89
  475.2 11.4 %copy-start.2 = (bf16[1,256,512]{2,1,0:T(8,128)(2,1)S(1)}, bf16[1,256,512]{2,1,0:T(8,128)(2,1)}, u32[]{:S(2)}) copy-start(bf16[1,256,512]{2,1,0:T(8,128)(2,1)} %copy-done.1) | copy-start | bytes 786436
  486.6 1.9 copy-start
Sparse Core Ops, SparseCore 0:
  451.4 40.2 reduce-scatter.2
  495.0 39.6 reduce-scatter.4
where the time goes:
time: 642 us; the launch traced here: 640 us
  blocking collectives  306 us (48%)
  other arithmetic  181 us (28%)
  local copies, waits for them, and re-layouts  124 us (19%)
  between operations  14.9 us (2%)
  matrix products  8.92 us (1%)
    unnamed x2, blocking collectives  277 us
    slice x1, other arithmetic, spread(): padded[:, :, tap_index, 2 - shift_depth:2 - shift_depth + SIDE, 2 - shift...  178 us
    unnamed x76, local copies, waits for them, and re-layouts  46.2 us
    all_gather x2, blocking collectives, all_channels(): return lax.all_gather(grad_maps, 'chan', axis=1, tiled=True)  28.6 us
    another operation x2, local copies, waits for them, and re-layouts  22.6 us
    reshape x1, local copies, waits for them, and re-layouts, spread(): cube_form = terms.reshape(batch_size, channels, 27, SIDE, SIDE, SIDE)  22.4 us
    another operation x4, local copies, waits for them, and re-layouts, shifted(): jnp.stack(shifted_views, axis=2)  20.4 us
  transfers between devices with their start and end apart: 3, of which 0 were waited for; matrix products, arithmetic and copies ran while one was open for 39% of the time, Pallas kernels for 0%

commit v1 on v0

--- a/solution.py
+++ b/solution.py
@@ -54,7 +54,20 @@
 
 
 def all_channels(grad_maps):
-    return lax.all_gather(grad_maps, "chan", axis=1, tiled=True)
+
+    def write_points(field, a_name):
+        u1 = lax.axis_size(a_name)
+        odd = lax.axis_index(a_name)
+        top, mid_arr, r1 = (u1, odd, field.shape[1])
+        y2, vec_out = (field, 1)
+        while vec_out < top:
+            y2 = jnp.concatenate(
+                [y2, lax.ppermute(y2, a_name, [(b, (b - vec_out) % top) for b in range(top)])], 1
+            )
+            vec_out = 2 * vec_out
+        return jnp.roll(y2, mid_arr * r1, 1)
+
+    return write_points(grad_maps, "chan")
 
 
 def body(snapshots, first_weight, second_weight, cotangent):

time: 642 us -> 613 us (0.955)
  blocking collectives: 306 us -> 281 us
  local copies, waits for them, and re-layouts: 124 us -> 103 us
  waiting for transfers between devices: 0.04 us -> 11.2 us
  starting transfers between devices: 6.36 us -> 13.1 us
    all_gather x2 -> x0, blocking collectives: 28.6 us -> none  [all_channels(): return lax.all_gather(grad_maps, 'chan', axis=1, tiled=True)]
    unnamed x76 -> x82, local copies, waits for them, and re-layouts: 46.2 us -> 29.2 us
    ppermute x0 -> x4, waiting for transfers between devices: none -> 11.1 us  [write_points(): lax.ppermute(y2, a_name, [(b, (b - vec_out) % top) for b in range(top)])]
    ppermute x0 -> x4, starting transfers between devices: none -> 9.73 us  [write_points(): lax.ppermute(y2, a_name, [(b, (b - vec_out) % top) for b in range(top)])]
  transfers between devices with their start and end apart: 3 -> 7, of which waited for: 0 -> 2; matrix products, arithmetic and copies ran while one was open for 39% -> 10% of each run, Pallas kernels for 0% -> 0%
where the time goes in v1:
time: 613 us; the launch traced here: 612 us
  blocking collectives  281 us (46%)
  other arithmetic  180 us (29%)
  local copies, waits for them, and re-layouts  103 us (17%)
  between operations  15.1 us (2%)
  starting transfers between devices  13.1 us (2%)
  waiting for transfers between devices  11.2 us (2%)
  matrix products  8.82 us (1%)
    unnamed x2, blocking collectives  281 us
    slice x1, other arithmetic, spread(): padded[:, :, tap_index, 2 - shift_depth:2 - shift_depth + SIDE, 2 - shift...  177 us
    unnamed x82, local copies, waits for them, and re-layouts  29.2 us
    another operation x2, local copies, waits for them, and re-layouts  22.6 us
    reshape x1, local copies, waits for them, and re-layouts, spread(): cube_form = terms.reshape(batch_size, channels, 27, SIDE, SIDE, SIDE)  22.4 us
    another operation x4, local copies, waits for them, and re-layouts, shifted(): jnp.stack(shifted_views, axis=2)  17.8 us
  transfers between devices with their start and end apart: 7, of which 2 were waited for; matrix products, arithmetic and copies ran while one was open for 10% of the time, Pallas kernels for 0%

profile of v1, /device:TPU:0, one launch (start us, length us, event | category | flops | bytes accessed | tf_op | source)
XLA Modules:
  0.0 612.1 jit_solution(15824838282711595184)
XLA Ops:
  7.2 5.1 collective-permute-start
  12.3 0.9 copy.71
  13.7 1.0 reduce.22
  15.4 3.3 all-to-all-start
  18.8 1.7 copy.63
  20.5 1.2 reshape.411
  24.5 2.8 collective-permute-start.1
  37.1 0.7 fusion.76
  46.0 9.5 %copy.58 = bf16[1,64,27,8,8,8]{2,1,5,4,3,0:T(8,128)(2,1)} copy(bf16[1,64,27,8,8,8]{1,5,4,3,2,0:T(8,128)(2,1)} %fusion.100) | data formatting | bytes 3538944 | tf_op jit(solution)/shard_map/stack | solution.py:25
  55.5 11.3 %reshape.407 = bf16[1728,512]{0,1:T(8,128)(2,1)S(1)} reshape(bf16[1,64,27,8,8,8]{2,1,5,4,3,0:T(8,128)(2,1)} %copy.58) | data formatting | bytes 3538944 | tf_op jit(solution)/shard_map/reshape.2
  66.8 1.2 copy-done.3
  69.1 143.3 %all-reduce.7 = bf16[1,256,512]{2,0,1:T(2,128)(2,1)S(1)} all-reduce(f32[1,256,512]{2,0,1:T(1,128)S(1)} %copy.60), channel_id=2, replica_groups=mesh['sample'=8,'chan'=4] {'chan'}, use_global_device_ids=true, to_apply=%region_0.1.clone | all-reduce | flops 131072 | bytes 786432
  212.5 0.8 copy.61
  213.3 1.0 fusion.46
  215.0 1.8 convolution_bitcast_fusion
  216.7 3.1 copy.65
  219.9 22.4 %reshape.413 = f32[1,64,27,8,8,8]{2,1,5,4,3,0:T(8,128)} reshape(f32[1,1728,512]{1,2,0:T(8,128)} %copy.65) | data formatting | bytes 7077888 | tf_op jit(solution)/shard_map/reshape | solution.py:30
  242.3 176.8 %fusion.16 = (f32[64,8,8,8]{0,3,2,1:T(8,128)S(1)}, f32[64,8,8,8]{0,3,2,1:T(8,128)S(1)}, f32[64,8,8,8]{0,3,2,1:T(8,128)S(1)}, f32[64,8,8,8]{0,3,2,1:T(8,128)S(1)}...) fusion(f32[1,64,27,8,8,8]{2,1,5,4,3,0:T(8,128)} %reshape.413), kind=kLoop, calls=%fused_computation.42 | loop fusion | flops 524288 | bytes 34996224 | tf_op jit(solution)/shard_map/slice | solution.py:37
  419.1 0.9 fusion.33
  421.4 7.6 %copy.62 = bf16[1,64,27,8,8,8]{2,1,5,4,3,0:T(8,128)(2,1)} copy(bf16[1,64,27,8,8,8]{1,5,4,3,2,0:T(8,128)(2,1)S(1)} %fusion.152) | data formatting | bytes 3538944 | tf_op jit(solution)/shard_map/stack | solution.py:25
  429.0 11.3 %reshape.410 = bf16[1728,512]{0,1:T(8,128)(2,1)S(1)} reshape(bf16[1,64,27,8,8,8]{2,1,5,4,3,0:T(8,128)(2,1)} %copy.62) | data formatting | bytes 3538944 | tf_op jit(solution)/shard_map/reshape.5
  440.3 1.9 fusion.155
  442.3 0.9 collective-permute-start.2
  443.2 5.4 collective-permute-done.2
  448.8 0.9 collective-permute-start.3
  449.7 5.7 collective-permute-done.3
  455.4 3.9 fusion.38
  460.3 137.4 %all-reduce.8 = bf16[1,256,512]{2,0,1:T(2,128)(2,1)S(1)} all-reduce(f32[1,256,512]{2,0,1:T(1,128)S(1)} %copy.64), channel_id=3, replica_groups=mesh['sample'=8,'chan'=4] {'chan'}, use_global_device_ids=true, to_apply=%region_1.2.clone | all-reduce | flops 131072 | bytes 786432
  598.5 2.2 reshape.416
  600.7 1.2 copy.68
  601.9 2.2 reshape.415
  604.1 1.2 copy.67
  (96 shorter events, 26.4 us)
Async XLA Ops:
  7.2 14.6 %copy-start.4 = (bf16[64,27,256]{2,0,1:T(8,128)(2,1)S(1)}, bf16[64,27,256]{2,0,1:T(8,128)(2,1)}, u32[]{:S(2)}) copy-start(bf16[64,27,256]{2,0,1:T(8,128)(2,1)} %param.7) | copy-start | bytes 2654212
  7.2 16.6 %collective-permute-start = (bf16[1,64,512]{2,1,0:T(8,128)(2,1)}, bf16[1,64,512]{2,1,0:T(8,128)(2,1)S(1)}, u32[]{:S(2)}, u32[]{:S(2)}) collective-permute-start(bf16[1,64,512]{2,1,0:T(8,128)(2,1)} %param.9), channel_id=1, source_target_pairs={{0,3},{1,0},{2,1},{3,2},{4,7},{5,4},{6,5},{7,6},{8,11},{9,8},{10,9... | collective-permute-start | bytes 196616 | tf_op jit(solution)/shard_map/ppermute | solution.py:65
  15.4 11.9 %all-to-all-start = ((bf16[4,2,4096]{2,1,0:T(2,128)(2,1)}), bf16[4,2,4096]{2,1,0:T(2,128)(2,1)S(1)}, u32[]{:S(2)}, u32[]{:S(2)}) async-start(bf16[4,2,4096]{2,1,0:T(2,128)(2,1)} %reshape.442), calls=%async_computation | async-start | bytes 131072 | tf_op jit(solution)/shard_map/all_to_all | solution.py:74
  18.7 579.8 %reduce-scatter.5.cloned.1.call-start = ((), (), s32[]{:S(2)}) async-start(), calls=%async_computation.4 | async-start | bytes 2064384 | tf_op jit(solution)/shard_map/reduce_scatter | solution.py:102
  18.8 3.8 copy-start.8
  18.8 5.0 copy-start.7
  24.5 188.8 %collective-permute-start.1 = (bf16[1,128,512]{2,1,0:T(8,128)(2,1)}, bf16[1,128,512]{2,1,0:T(8,128)(2,1)S(1)}, u32[]{:S(2)}, u32[]{:S(2)}) collective-permute-start(bf16[1,128,512]{2,1,0:T(8,128)(2,1)} %pad_maximum_fusion), channel_id=1, source_target_pairs={{0,2},{1,3},{2,0},{3,1},{4,6},{5,7},{6,4},{7,5},{8,10},{9,11},{10,... | collective-permute-start | bytes 393224 | tf_op jit(solution)/shard_map/ppermute | solution.py:65
  66.8 1.2 copy-start.3
  214.2 0.7 copy-start.1
  242.3 176.8 %copy-start.6 = (bf16[1,64,512]{1,2,0:T(8,128)(2,1)S(1)}, bf16[1,64,512]{1,2,0:T(8,128)(2,1)}, u32[]{:S(2)}) copy-start(bf16[1,64,512]{1,2,0:T(8,128)(2,1)} %copy.61) | copy-start | bytes 196612
  429.0 11.4 %copy-start.2 = (bf16[256,512]{1,0:T(8,128)(2,1)S(1)}, bf16[256,512]{1,0:T(8,128)(2,1)}, u32[]{:S(2)}) copy-start(bf16[256,512]{1,0:T(8,128)(2,1)} %copy-done.1) | copy-start | bytes 786436
  440.3 2.0 copy-start.5
  442.2 159.7 %reduce-scatter.3.cloned.1.call-start = ((), (), s32[]{:S(2)}) async-start(), calls=%async_computation.3 | async-start | bytes 2064384 | tf_op jit(solution)/shard_map/reduce_scatter | solution.py:101
  442.3 6.3 %collective-permute-start.2 = (bf16[1,64,512]{1,2,0:T(8,128)(2,1)S(1)}, bf16[1,64,512]{1,2,0:T(8,128)(2,1)S(1)}, u32[]{:S(2)}, u32[]{:S(2)}) collective-permute-start(bf16[1,64,512]{1,2,0:T(8,128)(2,1)S(1)} %copy-done.5), channel_id=1, source_target_pairs={{0,3},{1,0},{2,1},{3,2},{4,7},{5,4},{6,5},{7,6},{8,11},{9,8},{10,9... | collective-permute-start | bytes 196616 | tf_op jit(solution)/shard_map/ppermute | solution.py:65
  448.7 10.5 %copy-start = (bf16[1728,256]{1,0:T(8,128)(2,1)S(1)}, bf16[1728,256]{1,0:T(8,128)(2,1)}, u32[]{:S(2)}) copy-start(bf16[1728,256]{1,0:T(8,128)(2,1)} %reshape.411) | copy-start | bytes 2654212
  448.8 6.6 %collective-permute-start.3 = (bf16[1,128,512]{1,2,0:T(8,128)(2,1)S(1)}, bf16[1,128,512]{1,2,0:T(8,128)(2,1)S(1)}, u32[]{:S(2)}, u32[]{:S(2)}) collective-permute-start(bf16[1,128,512]{1,2,0:T(8,128)(2,1)S(1)} %pad_maximum_fusion.1), channel_id=1, source_target_pairs={{0,2},{1,3},{2,0},{3,1},{4,6},{5,7},{6,4},{7,5},{8,10},{9,11},{10,... | collective-permute-start | bytes 393224 | tf_op jit(solution)/shard_map/ppermute | solution.py:65
Sparse Core Ops, SparseCore 0:
  442.4 38.5 reduce-scatter.4
  484.3 39.6 reduce-scatter.2
